TPU v7x, 32 devices: a whole 2x2x4 slice. The times are simulated.
32 devices in a mesh: fsdp: 4 (over z), tp: 8 (over y, x, core).
Axes of the slice: x: 2, y: 2, z: 4, core: 2. Of those that a mesh axis runs over, the one named last changes fastest.
Arguments:
- tokens: bfloat16 [8192, 2048], P(('fsdp', 'tp')), may hold values from -6 to 6
- seq_len: int32 [8], replicated, may hold values from 256 to 1792, as said below
- seq_group: int32 [8], replicated, may hold values from 0 to 3, as said below
- ln1_gain: float32 [2048], replicated, may hold values from 0.1 to 1.9
- ln1_bias: float32 [2048], replicated, may hold values from -1.75 to 1.75
- qkv_weight: bfloat16 [2048, 3, 2048], P('fsdp', None, 'tp'), may hold values from -0.125 to 0.125
- qv_bias: float32 [2, 2048], P(None, 'tp'), may hold values from -0.625 to 0.625
- out_weight: bfloat16 [2048, 2048], P('tp', 'fsdp'), may hold values from -0.75 to 0.75
- out_bias: float32 [2048], replicated, may hold values from -1.75 to 1.75
- ln2_gain: float32 [2048], replicated, may hold values from 0.1 to 1.9
- ln2_bias: float32 [2048], replicated, may hold values from -1.75 to 1.75
- up_weight: bfloat16 [2048, 8192], P('fsdp', 'tp'), may hold values from -0.125 to 0.125
- up_bias: float32 [8192], P('tp'), may hold values from -1.75 to 1.75
- down_weight: bfloat16 [8192, 2048], P('tp', 'fsdp'), may hold values from -0.0625 to 0.0625
- down_bias: float32 [2048], replicated, may hold values from -1.75 to 1.75
- out_grad: bfloat16 [8192, 2048], P(('fsdp', 'tp')), may hold values from -6 to 6
Outputs:
- layer_out: bfloat16 [8192, 2048], P(('fsdp', 'tp'))
- tokens_grad: bfloat16 [8192, 2048], P(('fsdp', 'tp'))
- grad_ln1_gain: float32 [2048], replicated
- grad_ln1_bias: float32 [2048], replicated
- grad_qkv_weight: float32 [2048, 3, 2048], P('fsdp', None, 'tp')
- grad_qv_bias: float32 [2, 2048], P(None, 'tp')
- grad_out_weight: float32 [2048, 2048], P('tp', 'fsdp')
- grad_out_bias: float32 [2048], replicated
- grad_ln2_gain: float32 [2048], replicated
- grad_ln2_bias: float32 [2048], replicated
- grad_up_weight: float32 [2048, 8192], P('fsdp', 'tp')
- grad_up_bias: float32 [8192], P('tp')
- grad_down_weight: float32 [8192, 2048], P('tp', 'fsdp')
- grad_down_bias: float32 [2048], replicated
Inputs may be any that keep to these rules, and one draw needn't show every extreme that they name: `seq_group`: every group holds exactly two sequences. `seq_len`: every length is a multiple of 256; the two sequences of a group take at most 2048 rows together, and in every draw some group is filled exactly.
All inputs are finite; a program needn't handle non-finite values.
Results may differ from a plain program's by a relative error of at most 0.02.
Values may be sent and summed in bfloat16 or wider, within the bound.
No kernel may reach another device: no remote copies, remote signals or barrier semaphores. Data moves between devices by JAX's collectives and lax.ppermute only.
A program may use at most 192 MiB of HBM per device.

v0:
```python
import jax
import jax.numpy as jnp
from jax import lax
from jax.experimental import pallas as pl
from jax.experimental.pallas import tpu as pltpu
from jax.sharding import PartitionSpec as P


HEAD_DIM = 128


EPSILON = 1e-05
MASKED = -1e30


def layer_norm(values, gain_vec, bias_vec):
    row_mean = jnp.mean(values, axis=-1, keepdims=True)
    centred = values - row_mean
    variance = jnp.mean(centred * centred, axis=-1, keepdims=True)
    return centred * lax.rsqrt(variance + EPSILON) * gain_vec + bias_vec


def gelu_pair(values):
    squared = values * values
    bent = jnp.tanh(GELU_RATE * values * (1.0 + GELU_CUBE * squared))
    upper = 0.5 * (1.0 + bent)
    slope = upper + 0.5 * values * (1.0 - bent * bent) * GELU_RATE * (1.0 + 3.0 * GELU_CUBE * squared)
    return values * upper, slope


def contract_rows(left, right):
    return lax.dot_general(
        left, right, (((0,), (0,)), ((), ())), preferred_element_type=jnp.float32
    )


def contract_cols(left, right):
    return lax.dot_general(
        left, right, (((1,), (1,)), ((), ())), preferred_element_type=jnp.float32
    )


SWAP_TP = 8
BLOCK = 256
LOG2_E = 1.4426950408889634
GELU_RATE = 0.7978845608028654
GELU_CUBE = 0.044715


def exchange(piece, mask):
    return lax.ppermute(piece, "tp", [(at, at ^ mask) for at in range(SWAP_TP)])


def tie(*values):
    return lax.optimization_barrier(values)


def gather_first(piece):
    if lax.axis_size("tp") != SWAP_TP:
        return (lax.all_gather(piece, "tp", axis=0, tiled=True),)
    return piece, exchange(piece, 2), exchange(piece, 4), exchange(piece, 1)


def gather_second(state):
    if len(state) == 1:
        return state
    piece, from_x, from_y, own_twin = state
    half = piece.shape[0] // 2
    far_low = exchange(from_x[:half], 4)
    far_high = exchange(from_y[half:], 2)
    return piece, from_x, from_y, far_low, far_high, own_twin, exchange(from_x, 1), exchange(from_y, 1)


def gather_pieces(state):
    if len(state) == 1:
        return state
    far_low, far_high = state[3:5]
    return (*state, exchange(far_low, 1), exchange(far_high, 1))


def gather_last(state):
    return jnp.concatenate(gather_pieces(state), axis=0) if len(state) > 1 else state[0]


def gather_rows(piece):
    return gather_last(gather_second(gather_first(piece)))


def add_low(left, right):
    return (left.astype(jnp.float32) + right.astype(jnp.float32)).astype(jnp.bfloat16)


def scatter_pair(left, multiply, first, count):
    if lax.axis_size("tp") != SWAP_TP:
        return multiply(left)
    rows = left.shape[0] // SWAP_TP
    twin = multiply(left[(4 + first) * rows : (4 + first + count) * rows])
    return add_low(multiply(left[first * rows : (first + count) * rows]), exchange(twin, 1))


def scatter_multiply(left, multiply):
    if lax.axis_size("tp") != SWAP_TP:
        return (scatter_pair(left, multiply, 0, 0),)
    return tuple(scatter_pair(left, multiply, first, count) for first, count in ((3, 1), (1, 2), (0, 1)))


def scatter_pieces(parts):
    if len(parts) == 1:
        return parts
    far, mixed, home = parts
    rows = far.shape[0]
    half = rows // 2
    to_x, to_y = mixed[:rows], mixed[rows:]
    return far[:half], far[half:], to_x[:half], to_y[half:], to_x[half:], to_y[:half], home


def scatter_send(pieces):
    if len(pieces) == 1:
        return (lax.psum_scatter(pieces[0], "tp", scatter_dimension=0, tiled=True),)
    far_low, far_high, x_low, y_high, *kept = pieces
    return (
        exchange(far_low, 2),
        exchange(far_high, 4),
        exchange(x_low, 2),
        exchange(y_high, 4),
        *kept,
    )


def scatter_first(parts):
    return scatter_send(scatter_pieces(parts))


def scatter_second(state):
    if len(state) == 1:
        return state
    far_low, far_high, x_low, y_high, to_x, to_y, home = state
    return (
        x_low,
        exchange(add_low(to_x, far_high), 2),
        exchange(add_low(to_y, far_low), 4),
        y_high,
        home,
    )


def scatter_last(state):
    if len(state) == 1:
        return state[0].astype(jnp.float32)
    x_low, x_high, y_low, y_high, home = (part.astype(jnp.float32) for part in state)
    return (
        home
        + jnp.concatenate([x_low, x_high], axis=0)
        + jnp.concatenate([y_low, y_high], axis=0)
    )


def sum_direct(vector, axis, steps):
    count = lax.axis_size(axis)
    terms = [vector] + [
        lax.ppermute(vector, axis, [(at, at ^ step) for at in range(count)]) for step in steps
    ]
    while len(terms) > 1:
        terms = [terms[at] + terms[at + 1] for at in range(0, len(terms), 2)]
    return terms[0]


def sum_fsdp(vector):
    return sum_direct(vector, "fsdp", range(1, lax.axis_size("fsdp")))


def sum_tp(vector):
    return sum_direct(
        sum_direct(vector, "tp", (1,)), "tp", range(2, lax.axis_size("tp"), 2)
    )


def block_table(seq_len, seq_group, group_id, block_count):
    seq_order = jnp.arange(seq_len.shape[0], dtype=jnp.int32)
    same_before = (seq_group[None, :] == seq_group[:, None]) & (
        seq_order[None, :] < seq_order[:, None]
    )
    starts = jnp.sum(jnp.where(same_before, seq_len[None, :], 0), axis=1) // BLOCK
    ends = starts + seq_len // BLOCK
    block_at = jnp.arange(block_count, dtype=jnp.int32)
    inside = (
        (seq_group[None, :] == group_id)
        & (starts[None, :] <= block_at[:, None])
        & (block_at[:, None] < ends[None, :])
    )
    held = jnp.sum(inside.astype(jnp.int32), axis=1)
    first = jnp.sum(jnp.where(inside, starts[None, :], 0), axis=1)
    first = jnp.where(held > 0, first, block_at)
    place = block_at
    if lax.axis_size("tp") == SWAP_TP:
        apart = block_at ^ lax.axis_index("tp")
        place = (apart >> 1) + 4 * (apart & 1)
    return jnp.stack([place, first, held]).astype(jnp.int32)


def dot_nt(left, right):
    return lax.dot_general(
        left, right, (((1,), (1,)), ((), ())), preferred_element_type=jnp.float32
    )


def block_rows(place):
    return pl.ds(pl.multiple_of(place * BLOCK, BLOCK), BLOCK)


def attend_kernel(table, qkv, ctx, lse):
    head_cols = ctx.shape[1]
    heads = head_cols // HEAD_DIM
    sharpness = HEAD_DIM ** (-0.5) * LOG2_E
    key_row = lax.broadcasted_iota(jnp.int32, (BLOCK, BLOCK), 0)
    query_col = lax.broadcasted_iota(jnp.int32, (BLOCK, BLOCK), 1)

    def cols(part, head):
        return pl.ds(part * head_cols + head * HEAD_DIM, HEAD_DIM)

    def query_block(at, _):
        rows = block_rows(table[0, at])
        queries = [qkv[rows, cols(0, head)] for head in range(heads)]
        allowed = (key_row == query_col) | ((key_row < query_col) & (table[2, at] > 0))

        def start(head):
            scores = dot_nt(qkv[rows, cols(1, head)], queries[head]) * sharpness
            scores = jnp.where(allowed, scores, MASKED)
            top = jnp.max(scores, axis=0, keepdims=True)
            weights = jnp.exp2(scores - top)
            total = jnp.sum(weights, axis=0, keepdims=True)
            return top, total, contract_rows(qkv[rows, cols(2, head)], weights.astype(jnp.bfloat16))

        def key_block(key_at, carried):
            key_rows = block_rows(table[0, key_at])
            result = []
            for head in range(heads):
                top, total, mixed = carried[head]
                scores = dot_nt(qkv[key_rows, cols(1, head)], queries[head]) * sharpness
                new_top = jnp.maximum(top, jnp.max(scores, axis=0, keepdims=True))
                shrink = jnp.exp2(top - new_top)
                weights = jnp.exp2(scores - new_top)
                total = total * shrink + jnp.sum(weights, axis=0, keepdims=True)
                mixed = mixed * shrink + contract_rows(
                    qkv[key_rows, cols(2, head)], weights.astype(jnp.bfloat16)
                )
                result.append((new_top, total, mixed))
            return tuple(result)

        done = lax.fori_loop(
            table[1, at], at, key_block, tuple(start(head) for head in range(heads))
        )
        for head in range(heads):
            top, total, mixed = done[head]
            ctx[rows, pl.ds(head * HEAD_DIM, HEAD_DIM)] = (mixed / total).T.astype(jnp.bfloat16)
            lse[pl.ds(head * 8, 8), rows] = jnp.broadcast_to(top + jnp.log2(total), (8, BLOCK))
        return 0

    lax.fori_loop(0, table.shape[1], query_block, 0)


def attend_back_kernel(table, qkv, ctx, ctx_grad, lse, qkv_grad, sums, key_acc, value_acc):
    head_cols = ctx.shape[1]
    heads = head_cols // HEAD_DIM
    scaling = HEAD_DIM ** (-0.5)
    sharpness = scaling * LOG2_E
    key_row = lax.broadcasted_iota(jnp.int32, (BLOCK, BLOCK), 0)
    query_col = lax.broadcasted_iota(jnp.int32, (BLOCK, BLOCK), 1)
    sums[...] = jnp.zeros_like(sums)

    def cols(part, head):
        return pl.ds(part * head_cols + head * HEAD_DIM, HEAD_DIM)

    def query_block(at, _):
        rows = block_rows(table[0, at])
        queries, grads, levels, dots = [], [], [], []
        for head in range(heads):
            own = pl.ds(head * HEAD_DIM, HEAD_DIM)
            queries.append(qkv[rows, cols(0, head)])
            grads.append(ctx_grad[rows, own])
            levels.append(lse[pl.ds(head * 8, 1), rows])
            dot = jnp.sum(
                grads[head].astype(jnp.float32) * ctx[rows, own].astype(jnp.float32),
                axis=-1,
                keepdims=True,
            )
            dots.append(jnp.broadcast_to(dot, (BLOCK, HEAD_DIM)).T[:1])
        allowed = (key_row == query_col) | ((key_row < query_col) & (table[2, at] > 0))

        def tile(head, key_rows, masked):
            keys = qkv[key_rows, cols(1, head)]
            probs = jnp.exp2(dot_nt(keys, queries[head]) * sharpness - levels[head])
            if masked:
                probs = jnp.where(allowed, probs, 0.0)
            prob_grad = dot_nt(qkv[key_rows, cols(2, head)], grads[head])
            score_grad = (probs * (prob_grad - dots[head])).astype(jnp.bfloat16)
            value_part = jnp.dot(
                probs.astype(jnp.bfloat16), grads[head], preferred_element_type=jnp.float32
            )
            key_part = jnp.dot(score_grad, queries[head], preferred_element_type=jnp.float32)
            return contract_rows(score_grad, keys), key_part, value_part

        query_acc = []
        for head in range(heads):
            own = pl.ds(head * HEAD_DIM, HEAD_DIM)
            query_part, key_part, value_part = tile(head, rows, True)
            key_acc[rows, own] = key_part
            value_acc[rows, own] = value_part
            query_acc.append(query_part)

        def key_block(key_at, carried):
            key_rows = block_rows(table[0, key_at])
            result = []
            for head in range(heads):
                own = pl.ds(head * HEAD_DIM, HEAD_DIM)
                query_part, key_part, value_part = tile(head, key_rows, False)
                key_acc[key_rows, own] += key_part
                value_acc[key_rows, own] += value_part
                result.append(carried[head] + query_part)
            return tuple(result)

        query_acc = lax.fori_loop(table[1, at], at, key_block, tuple(query_acc))
        for head in range(heads):
            low = (query_acc[head] * scaling).astype(jnp.bfloat16)
            qkv_grad[rows, cols(0, head)] = low
            sums[:1, pl.ds(head * HEAD_DIM, HEAD_DIM)] += jnp.sum(
                low.astype(jnp.float32), axis=0, keepdims=True
            )
        return 0

    lax.fori_loop(0, table.shape[1], query_block, 0)

    def finish(at, _):
        rows = block_rows(at)
        key_low = (key_acc[rows, :] * scaling).astype(jnp.bfloat16)
        value_low = value_acc[rows, :].astype(jnp.bfloat16)
        qkv_grad[rows, pl.ds(head_cols, head_cols)] = key_low
        qkv_grad[rows, pl.ds(2 * head_cols, head_cols)] = value_low
        sums[1:2, :] += jnp.sum(value_low.astype(jnp.float32), axis=0, keepdims=True)
        return 0

    lax.fori_loop(0, table.shape[1], finish, 0)


def whole_specs(count):
    return [pl.BlockSpec(memory_space=pltpu.VMEM) for _ in range(count)]


def attend(table, qkv_rows, head_cols):
    rows = qkv_rows.shape[0]
    heads = head_cols // HEAD_DIM
    return pl.pallas_call(
        attend_kernel,
        out_shape=(
            jax.ShapeDtypeStruct((rows, head_cols), jnp.bfloat16),
            jax.ShapeDtypeStruct((8 * heads, rows), jnp.float32),
        ),
        in_specs=[pl.BlockSpec(memory_space=pltpu.SMEM), *whole_specs(1)],
        out_specs=tuple(whole_specs(2)),
        name="attend",
    )(table, qkv_rows)


def attend_back(table, qkv_rows, context, ctx_grad, lse):
    rows, head_cols = context.shape
    return pl.pallas_call(
        attend_back_kernel,
        out_shape=(
            jax.ShapeDtypeStruct(qkv_rows.shape, jnp.bfloat16),
            jax.ShapeDtypeStruct((8, head_cols), jnp.float32),
        ),
        in_specs=[pl.BlockSpec(memory_space=pltpu.SMEM), *whole_specs(4)],
        out_specs=tuple(whole_specs(2)),
        scratch_shapes=[
            pltpu.VMEM((rows, head_cols), jnp.float32),
            pltpu.VMEM((rows, head_cols), jnp.float32),
        ],
        name="attend_back",
    )(table, qkv_rows, context, ctx_grad, lse)


def project_back_kernel(*refs):
    *pieces, context, out_full, ctx_grad, out_acc, context_turned, out_turned = refs
    context_turned[...] = context[...].T
    out_turned[...] = out_full[...].T
    spans, first = [], 0
    for piece in pieces:
        spans.append(pl.ds(first, piece.shape[0]))
        first += piece.shape[0]
    for piece, span in zip(pieces, spans):
        ctx_grad[span, :] = jnp.dot(
            piece[...], out_turned[...], preferred_element_type=jnp.float32
        ).astype(jnp.bfloat16)

    def tile(at, _):
        cols = pl.ds(pl.multiple_of(at * BLOCK, BLOCK), BLOCK)
        total = 0.0
        for piece, span in zip(pieces, spans):
            total = total + jnp.dot(
                context_turned[:, span], piece[:, cols], preferred_element_type=jnp.float32
            )
        out_acc[:, cols] = total.astype(jnp.bfloat16)
        return 0

    lax.fori_loop(0, out_acc.shape[1] // BLOCK, tile, 0)


def project_back(pieces, context, out_full):
    return pl.pallas_call(
        project_back_kernel,
        out_shape=(
            jax.ShapeDtypeStruct(context.shape, jnp.bfloat16),
            jax.ShapeDtypeStruct(out_full.shape, jnp.bfloat16),
        ),
        in_specs=whole_specs(len(pieces) + 2),
        out_specs=tuple(whole_specs(2)),
        scratch_shapes=[
            pltpu.VMEM(context.shape[::-1], jnp.bfloat16),
            pltpu.VMEM(out_full.shape[::-1], jnp.bfloat16),
        ],
        name="project_back",
    )(*pieces, context, out_full)


def layer(
    tokens,
    seq_len,
    seq_group,
    ln1_gain,
    ln1_bias,
    qkv_weight,
    qv_bias,
    out_weight,
    out_bias,
    ln2_gain,
    ln2_bias,
    up_weight,
    up_bias,
    down_weight,
    down_bias,
    out_grad,
):
    width = tokens.shape[1]
    head_cols = qkv_weight.shape[2]
    table = block_table(
        seq_len,
        seq_group,
        lax.axis_index("fsdp"),
        tokens.shape[0] * lax.axis_size("tp") // BLOCK,
    )

    def gather_weights():
        return (
            lax.all_gather(qkv_weight, "fsdp", axis=0, tiled=True),
            lax.all_gather(out_weight, "fsdp", axis=1, tiled=True),
            lax.all_gather(up_weight, "fsdp", axis=0, tiled=True),
            lax.all_gather(down_weight, "fsdp", axis=1, tiled=True),
        )

    def sum_weights(partial_sums, axis):
        return lax.psum_scatter(
            partial_sums, "fsdp", scatter_dimension=axis, tiled=True
        )

    inputs = tokens.astype(jnp.float32)
    norm1 = layer_norm(inputs, ln1_gain, ln1_bias).astype(jnp.bfloat16)
    qkv_full, out_full, up_full, down_full = gather_weights()
    qkv_flat = qkv_full.reshape(width, 3 * head_cols)
    qkv_shift = jnp.concatenate([qv_bias[0], jnp.zeros_like(qv_bias[0]), qv_bias[1]])
    norm1_rows = gather_rows(norm1)
    later_grad, norm1_rows = tie(out_grad, norm1_rows)
    grad_state = gather_first(later_grad)
    qkv_rows = (
        jnp.dot(norm1_rows, qkv_flat, preferred_element_type=jnp.float32) + qkv_shift
    ).astype(jnp.bfloat16)
    grad_state, qkv_rows = tie(grad_state, qkv_rows)
    grad_state = gather_second(grad_state)
    context, lse = attend(table, qkv_rows, head_cols)
    grad_state, context = tie(grad_state, context)

    attn_parts = scatter_multiply(
        context,
        lambda part: jnp.dot(part, out_full, preferred_element_type=jnp.float32).astype(
            jnp.bfloat16
        ),
    )
    attn_rows = scatter_last(scatter_second(scatter_first(attn_parts)))
    middle = inputs + attn_rows + out_bias
    norm2 = layer_norm(middle, ln2_gain, ln2_bias).astype(jnp.bfloat16)
    norm2_state = gather_first(norm2)
    grad_piece, norm2_state = tie(gather_last(grad_state), norm2_state)
    norm_piece = gather_last(gather_second(norm2_state))
    pre = jnp.dot(norm_piece, up_full, preferred_element_type=jnp.float32) + up_bias
    act_value, slope = gelu_pair(pre)
    act_rows, slope = tie(act_value.astype(jnp.bfloat16), slope.astype(jnp.bfloat16))

    down_acc = contract_rows(act_rows, grad_piece).astype(jnp.bfloat16)
    down_full, down_acc = tie(down_full, down_acc)
    act_grad = contract_cols(grad_piece, down_full)
    pre_grad = (act_grad * slope.astype(jnp.float32)).astype(jnp.bfloat16)
    shift_acc = jnp.sum(pre_grad.astype(jnp.float32), axis=0)
    norm2_grad_state = scatter_first(
        scatter_multiply(
            pre_grad, lambda part: contract_cols(part, up_full).astype(jnp.bfloat16)
        )
    )
    up_acc = contract_rows(norm_piece, pre_grad).astype(jnp.bfloat16)
    norm2_grad_state, up_acc = tie(norm2_grad_state, up_acc)
    norm2_grad = scatter_last(scatter_second(norm2_grad_state))
    _, ln2_back = jax.vjp(layer_norm, middle, ln2_gain, ln2_bias)
    middle_ln, grad_g2, grad_b2 = ln2_back(norm2_grad)
    grad_rows = out_grad.astype(jnp.float32)
    middle_grad = grad_rows + middle_ln
    portion_state = gather_first(middle_grad.astype(jnp.bfloat16))
    last_part, act_rows = tie(portion_state[-1], act_rows)
    portion_state = (*portion_state[:-1], last_part)
    mlp_pieces = scatter_pieces(
        scatter_multiply(
            act_rows,
            lambda part: jnp.dot(part, down_full, preferred_element_type=jnp.float32).astype(
                jnp.bfloat16
            ),
        )
    )
    portion_state, mlp_pieces = tie(portion_state, mlp_pieces)
    portion = gather_pieces(gather_second(portion_state))
    shard_down = sum_weights(down_acc, 1)
    portion, mlp_pieces, shard_down = tie(portion, mlp_pieces, shard_down)
    mlp_state = scatter_send(mlp_pieces)
    ctx_grad, out_acc = project_back(portion, context, out_full)
    shard_out = sum_weights(out_acc, 1)
    qkv_grad, qv_sums = attend_back(table, qkv_rows, context, ctx_grad, lse)
    mlp_state, qkv_grad = tie(mlp_state, qkv_grad)
    mlp_state = scatter_second(mlp_state)
    shard_up = sum_weights(up_acc, 0)

    def norm1_multiply(part):
        return contract_cols(part, qkv_flat).astype(jnp.bfloat16)

    split = lax.axis_size("tp") == SWAP_TP
    if split:
        far = scatter_pair(qkv_grad, norm1_multiply, 3, 1)
        far, qkv_grad = tie(far, qkv_grad)
        mixed = scatter_pair(qkv_grad, norm1_multiply, 1, 2)
        mixed, qkv_grad = tie(mixed, qkv_grad)
        *norm1_state, home = scatter_send(scatter_pieces((far, mixed, mixed)))
    else:
        norm1_state = list(scatter_first(scatter_multiply(qkv_grad, norm1_multiply)))
    grad_qkv_w = contract_rows(qkv_grad, norm1_rows).astype(jnp.bfloat16)
    grad_qkv_w, qkv_grad, shard_up = tie(grad_qkv_w, qkv_grad, shard_up)
    norm1_state, qkv_grad, mlp_state = tie(norm1_state, qkv_grad, mlp_state)
    if split:
        norm1_state = (*norm1_state, scatter_pair(qkv_grad, norm1_multiply, 0, 1))
    norm1_state = tuple(norm1_state)
    layer_out = (middle + scatter_last(mlp_state) + down_bias).astype(jnp.bfloat16)
    norm1_state, shard_out = tie(norm1_state, shard_out)
    norm1_grad = scatter_last(scatter_second(norm1_state))
    shard_qkv = sum_weights(grad_qkv_w, 1).reshape(3, head_cols, -1).transpose(2, 0, 1)
    _, ln1_back = jax.vjp(layer_norm, inputs, ln1_gain, ln1_bias)
    input_ln, grad_g1, grad_b1 = ln1_back(norm1_grad)
    tokens_grad = (middle_grad + input_ln).astype(jnp.bfloat16)

    wide_sums = [
        jnp.sum(middle_grad, axis=0),
        grad_g2,
        grad_b2,
        jnp.sum(grad_rows, axis=0),
        grad_g1,
        grad_b1,
    ]
    summed = sum_fsdp(jnp.concatenate([*wide_sums, qv_sums[0], qv_sums[1], shift_acc]))
    wide = sum_tp(summed[: 6 * width]).reshape(6, width)
    own = summed[6 * width :]
    return (
        layer_out,
        tokens_grad,
        wide[4],
        wide[5],
        shard_qkv.astype(jnp.float32),
        own[: 2 * head_cols].reshape(2, head_cols),
        shard_out.astype(jnp.float32),
        wide[0],
        wide[1],
        wide[2],
        shard_up.astype(jnp.float32),
        own[2 * head_cols :],
        shard_down.astype(jnp.float32),
        wide[3],
    )


def solution(mesh):
    placed = (
        P(("fsdp", "tp"), None),
        P(),
        P(),
        P(),
        P(),
        P("fsdp", None, "tp"),
        P(None, "tp"),
        P("tp", "fsdp"),
        P(),
        P(),
        P(),
        P("fsdp", "tp"),
        P("tp"),
        P("tp", "fsdp"),
        P(),
        P(("fsdp", "tp"), None),
    )
    return jax.shard_map(
        layer,
        mesh=mesh,
        in_specs=placed,
        out_specs=(
            P(("fsdp", "tp"), None),
            P(("fsdp", "tp"), None),
            P(),
            P(),
            P("fsdp", None, "tp"),
            P(None, "tp"),
            P("tp", "fsdp"),
            P(),
            P(),
            P(),
            P("fsdp", "tp"),
            P("tp"),
            P("tp", "fsdp"),
            P(),
        ),
        check_vma=False,
    )
```

profile of v0, /device:TPU:0, one launch (start us, length us, event | category | flops | bytes accessed | tf_op | source)
XLA Modules:
  0.0 573.9 jit_solution(8863282000833951634)
XLA Ops:
  17.7 21.8 %collective-permute-done.1 = bf16[256,2048]{1,0:T(8,128)(2,1)S(1)} collective-permute-done((bf16[256,2048]{1,0:T(8,128)(2,1)}, bf16[256,2048]{1,0:T(8,128)(2,1)S(1)}, u32[]{:S(2)}, u32[]{:S(2)}) %collective-permute-start.1) | collective-permute-done | bytes 1048608 | tf_op jit(solution)/shard_map/ppermute | solution.py:51
  63.2 13.2 %all-gather.5.cloned.1.call-done = bf16[2048,3,256]{0,2,1:T(8,128)(2,1)} async-done(((bf16[512,3,256]{0,2,1:T(8,128)(2,1)}), bf16[2048,3,256]{0,2,1:T(8,128)(2,1)}) %all-gather.5.cloned.1.call-update) | async-done | bytes 3145744 | tf_op jit(solution)/shard_map/all_gather | solution.py:454
  76.4 11.3 %add_convert_fusion.1.qkv = bf16[2048,768]{1,0:T(8,128)(2,1)} fusion(f32[768]{0:T(1024)S(1)} %pad_maximum_fusion, bf16[2048,2048]{1,0:T(8,128)(2,1)} %constant_dynamic-update-slice_fusion, bf16[2048,768]{0,1:T(8,128)(2,1)} %bitcast.55), kind=kOutput, calls=%fused_computation.6 | convolution fusion | flops 6445596672 | bytes 14683136 | tf_op jit(solution)/shard_map/dot_general | solution.py:474
  94.9 16.2 %attend.1 = (bf16[2048,256]{1,0:T(8,128)(2,1)}, f32[16,2048]{1,0:T(8,128)}) custom-call(s32[3,8]{1,0:T(4,128)} %pad_add_fusion.table, bf16[2048,768]{1,0:T(8,128)(2,1)} %add_convert_fusion.1.qkv), custom_call_target="tpu_custom_call" | custom-call | tf_op jit(solution)/shard_map/attend/pallas_call | solution.py:352
  127.2 9.3 %collective-permute-done.22 = bf16[128,2048]{1,0:T(8,128)(2,1)S(1)} collective-permute-done((bf16[128,2048]{1,0:T(8,128)(2,1)S(1)}, bf16[128,2048]{1,0:T(8,128)(2,1)S(1)}, u32[]{:S(2)}, u32[]{:S(2)}) %collective-permute-start.22) | collective-permute-done | bytes 524320 | tf_op jit(solution)/shard_map/ppermute | solution.py:51
  143.7 8.2 %collective-permute-done.23 = bf16[128,2048]{1,0:T(8,128)(2,1)S(1)} collective-permute-done((bf16[128,2048]{1,0:T(8,128)(2,1)S(1)}, bf16[128,2048]{1,0:T(8,128)(2,1)S(1)}, u32[]{:S(2)}, u32[]{:S(2)}) %collective-permute-start.23) | collective-permute-done | bytes 524320 | tf_op jit(solution)/shard_map/ppermute | solution.py:51
  152.4 9.0 %collective-permute-done.24 = bf16[128,2048]{1,0:T(8,128)(2,1)S(1)} collective-permute-done((bf16[128,2048]{1,0:T(8,128)(2,1)S(1)}, bf16[128,2048]{1,0:T(8,128)(2,1)S(1)}, u32[]{:S(2)}, u32[]{:S(2)}) %collective-permute-start.24) | collective-permute-done | bytes 524320 | tf_op jit(solution)/shard_map/ppermute | solution.py:51
  170.4 19.7 %collective-permute-done.28 = bf16[256,2048]{1,0:T(8,128)(2,1)S(1)} collective-permute-done((bf16[256,2048]{1,0:T(8,128)(2,1)S(1)}, bf16[256,2048]{1,0:T(8,128)(2,1)S(1)}, u32[]{:S(2)}, u32[]{:S(2)}) %collective-permute-start.28) | collective-permute-done | bytes 1048608 | tf_op jit(solution)/shard_map/ppermute | solution.py:51
  197.1 10.0 %collective-permute-done.30 = bf16[128,2048]{1,0:T(8,128)(2,1)S(1)} collective-permute-done((bf16[128,2048]{1,0:T(8,128)(2,1)S(1)}, bf16[128,2048]{1,0:T(8,128)(2,1)S(1)}, u32[]{:S(2)}, u32[]{:S(2)}) %collective-permute-start.30) | collective-permute-done | bytes 524320 | tf_op jit(solution)/shard_map/ppermute | solution.py:51
  214.3 18.3 %add_convert_fusion = (bf16[2048,1024]{1,0:T(8,128)(2,1)}, bf16[2048,1024]{1,0:T(8,128)(2,1)S(1)}) fusion(f32[1024]{0:T(1024)S(1)} %copy-done.60, bf16[2048,2048]{1,0:T(8,128)(2,1)} %constant_dynamic-update-slice_fusion.20, bf16[2048,1024]{1,0:T(8,128)(2,1)} %all-gather.11.cloned.1.call-done), kind=kOutput, calls=%fused_computation.2 | convolution fusion | flops 8631877632 | bytes 20975616 | tf_op jit(solution)/shard_map/dot_general | solution.py:493
  234.6 11.0 %convolution_convert_fusion = bf16[1024,2048]{1,0:T(8,128)(2,1)} fusion(bf16[2048,1024]{1,0:T(8,128)(2,1)S(1)} %get-tuple-element.152, bf16[2048,2048]{1,0:T(8,128)(2,1)S(1)} %copy-done.39), kind=kOutput, calls=%fused_computation.11 | convolution fusion | flops 8592031744 | bytes 16777216 | tf_op jit(solution)/shard_map/dot_general | solution.py:32
  245.6 21.4 %all-gather.9.cloned.1.call-done = bf16[1024,2048]{1,0:T(8,128)(2,1)} async-done(((bf16[1024,512]{1,0:T(8,128)(2,1)}), bf16[1024,2048]{1,0:T(8,128)(2,1)}) %all-gather.9.cloned.1.call-update) | async-done | bytes 4194320 | tf_op jit(solution)/shard_map/all_gather | solution.py:457
  267.0 13.5 %convert_reduce_fusion = (f32[1024]{0:T(1024)S(1)}, bf16[2048,1024]{1,0:T(8,128)(2,1)S(1)}) fusion(bf16[2048,1024]{1,0:T(8,128)(2,1)} %get-tuple-element.143, bf16[2048,2048]{1,0:T(8,128)(2,1)} %copy-done.38, bf16[1024,2048]{1,0:T(8,128)(2,1)} %all-gather.9.cloned.1.call-done), kind=kOutput, calls=%fused_computation | convolution fusion | flops 8600419328 | bytes 20975616 | tf_op jit(solution)/shard_map/dot_general | solution.py:38
  304.7 13.3 %convolution_convert_fusion.1 = bf16[2048,1024]{1,0:T(8,128)(2,1)} fusion(bf16[2048,2048]{1,0:T(8,128)(2,1)} %constant_dynamic-update-slice_fusion.20, bf16[2048,1024]{1,0:T(8,128)(2,1)S(1)} %copy-done.64), kind=kOutput, calls=%fused_computation.12 | convolution fusion | flops 8592031744 | bytes 16777216 | tf_op jit(solution)/shard_map/dot_general | solution.py:32
  327.6 10.4 %collective-permute-done.44 = bf16[128,2048]{1,0:T(8,128)(2,1)S(1)} collective-permute-done((bf16[128,2048]{1,0:T(8,128)(2,1)S(1)}, bf16[128,2048]{1,0:T(8,128)(2,1)S(1)}, u32[]{:S(2)}, u32[]{:S(2)}) %collective-permute-start.44) | collective-permute-done | bytes 524320 | tf_op jit(solution)/shard_map/ppermute | solution.py:51
  369.2 14.2 %collective-permute-done.46.refs_2_ = bf16[256,2048]{1,0:T(8,128)(2,1)S(1)} collective-permute-done((bf16[256,2048]{1,0:T(8,128)(2,1)S(1)}, bf16[256,2048]{1,0:T(8,128)(2,1)S(1)}, u32[]{:S(2)}, u32[]{:S(2)}) %collective-permute-start.46) | collective-permute-done | bytes 1048608 | tf_op jit(solution)/shard_map/ppermute | solution.py:51
  387.4 10.6 %collective-permute-done.52.refs_4_ = bf16[128,2048]{1,0:T(8,128)(2,1)S(1)} collective-permute-done((bf16[128,2048]{1,0:T(8,128)(2,1)S(1)}, bf16[128,2048]{1,0:T(8,128)(2,1)S(1)}, u32[]{:S(2)}, u32[]{:S(2)}) %collective-permute-start.52) | collective-permute-done | bytes 524320 | tf_op jit(solution)/shard_map/ppermute | solution.py:51
  406.0 11.6 %project_back.1 = (bf16[2048,256]{1,0:T(8,128)(2,1)}, bf16[256,2048]{1,0:T(8,128)(2,1)}) custom-call(bf16[256,2048]{1,0:T(8,128)(2,1)} %copy-done.15, bf16[256,2048]{1,0:T(8,128)(2,1)} %copy-done.17, bf16[256,2048]{1,0:T(8,128)(2,1)} %copy-done.16, bf16[128,2048]{1,0:T(8,128)(2,1)} %copy-done.32, bf16[128,2048]{1,0:T(8,128)(2,1)} %copy-done.31, ...), custom_call_target="tpu_custom_call" | custom-call | tf_op jit(solution)/shard_map/project_back/pallas_call | solution.py:409
  417.7 18.9 %attend_back.1 = (bf16[2048,768]{1,0:T(8,128)(2,1)}, f32[8,256]{1,0:T(8,128)}) custom-call(s32[3,8]{1,0:T(4,128)} %pad_add_fusion.table, bf16[2048,768]{1,0:T(8,128)(2,1)} %add_convert_fusion.1.qkv, bf16[2048,256]{1,0:T(8,128)(2,1)} %get-tuple-element.127.refs_10_.ctx, bf16[2048,256]{1,0:T(8,128)(2,1)} %get-tuple-element.182.ctx_grad, ...), custom_call_target="tpu_custom_call" | custom-call | tf_op jit(solution)/shard_map/attend_back/pallas_call | solution.py:366
  468.2 10.7 %convolution_convert_fusion.2 = bf16[768,2048]{1,0:T(8,128)(2,1)} fusion(bf16[2048,768]{1,0:T(8,128)(2,1)S(1)} %copy-done.58, bf16[2048,2048]{1,0:T(8,128)(2,1)} %constant_dynamic-update-slice_fusion), kind=kOutput, calls=%fused_computation.13 | convolution fusion | flops 6444023808 | bytes 14680064 | tf_op jit(solution)/shard_map/dot_general | solution.py:32
  480.6 7.6 %collective-permute-done.66 = bf16[128,2048]{1,0:T(8,128)(2,1)S(1)} collective-permute-done((bf16[128,2048]{1,0:T(8,128)(2,1)}, bf16[128,2048]{1,0:T(8,128)(2,1)S(1)}, u32[]{:S(2)}, u32[]{:S(2)}) %collective-permute-start.66) | collective-permute-done | bytes 524320 | tf_op jit(solution)/shard_map/ppermute | solution.py:51
  508.4 9.5 %collective-permute-done.71 = bf16[128,2048]{1,0:T(8,128)(2,1)S(1)} collective-permute-done((bf16[128,2048]{1,0:T(8,128)(2,1)S(1)}, bf16[128,2048]{1,0:T(8,128)(2,1)S(1)}, u32[]{:S(2)}, u32[]{:S(2)}) %collective-permute-start.71) | collective-permute-done | bytes 524320 | tf_op jit(solution)/shard_map/ppermute | solution.py:51
  526.6 9.5 %collective-permute-start.73 = (f32[13824]{0:T(1024)S(1)}, f32[13824]{0:T(1024)S(1)}, u32[]{:S(2)}, u32[]{:S(2)}) collective-permute-start(f32[13824]{0:T(1024)S(1)} %constant_dynamic-update-slice_fusion.31), channel_id=1, source_target_pairs={{0,16},{8,24},{16,0},{24,8},{1,17},{9,25},{17,1},{25,9},{2,18},{10... | collective-permute-start | bytes 165896 | tf_op jit(solution)/shard_map/ppermute | solution.py:161
  536.1 10.7 %collective-permute-done.73 = f32[13824]{0:T(1024)S(1)} collective-permute-done((f32[13824]{0:T(1024)S(1)}, f32[13824]{0:T(1024)S(1)}, u32[]{:S(2)}, u32[]{:S(2)}) %collective-permute-start.73) | collective-permute-done | bytes 55328 | tf_op jit(solution)/shard_map/ppermute | solution.py:161
  (425 shorter events, 248.4 us)
Async XLA Ops:
  7.2 69.1 %all-gather.5.cloned.1.call-start = ((), (), s32[]{:S(2)}) async-start(), calls=%async_computation.4 | async-start | bytes 3932160 | tf_op jit(solution)/shard_map/all_gather | solution.py:454
  9.7 101.5 %all-gather.7.cloned.1.call-start = ((), (), s32[]{:S(2)}) async-start(), calls=%async_computation.5 | async-start | bytes 1310720 | tf_op jit(solution)/shard_map/all_gather | solution.py:455
  10.4 203.9 %all-gather.11.cloned.1.call-start = ((), (), s32[]{:S(2)}) async-start(), calls=%async_computation.7 | async-start | bytes 5242880 | tf_op jit(solution)/shard_map/all_gather | solution.py:456
  13.0 26.4 %collective-permute-start.1 = (bf16[256,2048]{1,0:T(8,128)(2,1)}, bf16[256,2048]{1,0:T(8,128)(2,1)S(1)}, u32[]{:S(2)}, u32[]{:S(2)}) collective-permute-start(bf16[256,2048]{1,0:T(8,128)(2,1)} %get-tuple-element.239), channel_id=1, source_target_pairs={{0,4},{1,5},{2,6},{3,7},{4,0},{5,1},{6,2},{7,3},{8,12},{9,13},{10,... | collective-permute-start | bytes 3145736 | tf_op jit(solution)/shard_map/ppermute | solution.py:51
  17.6 38.1 %collective-permute-start.4 = (bf16[256,2048]{1,0:T(8,128)(2,1)}, bf16[256,2048]{1,0:T(8,128)(2,1)S(1)}, u32[]{:S(2)}, u32[]{:S(2)}) collective-permute-start(bf16[256,2048]{1,0:T(8,128)(2,1)} %get-tuple-element.239), channel_id=1, source_target_pairs={{0,1},{1,0},{2,3},{3,2},{4,5},{5,4},{6,7},{7,6},{8,9},{9,8},{10,11... | collective-permute-start | bytes 3145736 | tf_op jit(solution)/shard_map/ppermute | solution.py:51
  17.6 249.5 %all-gather.9.cloned.1.call-start = ((), (), s32[]{:S(2)}) async-start(), calls=%async_computation.6 | async-start | bytes 5242880 | tf_op jit(solution)/shard_map/all_gather | solution.py:457
  60.6 27.0 %collective-permute-start.11 = (bf16[256,2048]{1,0:T(8,128)(2,1)S(1)}, bf16[256,2048]{1,0:T(8,128)(2,1)S(1)}, u32[]{:S(2)}, u32[]{:S(2)}) collective-permute-start(bf16[256,2048]{1,0:T(8,128)(2,1)S(1)} %copy-done.6), channel_id=1, source_target_pairs={{0,1},{1,0},{2,3},{3,2},{4,5},{5,4},{6,7},{7,6},{8,9},{9,8},{10,11... | collective-permute-start | bytes 3145736 | tf_op jit(solution)/shard_map/ppermute | solution.py:51
  61.1 26.5 %collective-permute-start.10 = (bf16[256,2048]{1,0:T(8,128)(2,1)S(1)}, bf16[256,2048]{1,0:T(8,128)(2,1)S(1)}, u32[]{:S(2)}, u32[]{:S(2)}) collective-permute-start(bf16[256,2048]{1,0:T(8,128)(2,1)S(1)} %copy-done.6), channel_id=1, source_target_pairs={{0,4},{1,5},{2,6},{3,7},{4,0},{5,1},{6,2},{7,3},{8,12},{9,13},{10,... | collective-permute-start | bytes 3145736 | tf_op jit(solution)/shard_map/ppermute | solution.py:51
  116.7 285.3 %reduce-scatter.5.cloned.1.call-start = ((), (), s32[]{:S(2)}) async-start(), calls=%async_computation.8 | async-start | bytes 5242880 | tf_op jit(solution)/shard_map/reduce_scatter | solution.py:461
  117.7 25.9 %collective-permute-start.16 = (bf16[256,2048]{1,0:T(8,128)(2,1)S(1)}, bf16[256,2048]{1,0:T(8,128)(2,1)S(1)}, u32[]{:S(2)}, u32[]{:S(2)}) collective-permute-start(bf16[256,2048]{1,0:T(8,128)(2,1)S(1)} %convolution_convert_fusion.21), channel_id=1, source_target_pairs={{0,1},{1,0},{2,3},{3,2},{4,5},{5,4},{6,7},{7,6},{8,9},{9,8},{10,11... | collective-permute-start | bytes 3145736 | tf_op jit(solution)/shard_map/ppermute | solution.py:51
  143.6 26.6 %collective-permute-start.25 = (bf16[128,2048]{1,0:T(8,128)(2,1)}, bf16[128,2048]{1,0:T(8,128)(2,1)S(1)}, u32[]{:S(2)}, u32[]{:S(2)}) collective-permute-start(bf16[128,2048]{1,0:T(8,128)(2,1)} %collective-permute-done.12), channel_id=1, source_target_pairs={{0,1},{1,0},{2,3},{3,2},{4,5},{5,4},{6,7},{7,6},{8,9},{9,8},{10,11... | collective-permute-start | bytes 1572872 | tf_op jit(solution)/shard_map/ppermute | solution.py:51
  164.5 25.6 %collective-permute-start.28 = (bf16[256,2048]{1,0:T(8,128)(2,1)S(1)}, bf16[256,2048]{1,0:T(8,128)(2,1)S(1)}, u32[]{:S(2)}, u32[]{:S(2)}) collective-permute-start(bf16[256,2048]{1,0:T(8,128)(2,1)S(1)} %add_convert_fusion.10), channel_id=1, source_target_pairs={{0,4},{1,5},{2,6},{3,7},{4,0},{5,1},{6,2},{7,3},{8,12},{9,13},{10,... | collective-permute-start | bytes 3145736 | tf_op jit(solution)/shard_map/ppermute | solution.py:51
  166.1 25.2 %collective-permute-start.27 = (bf16[256,2048]{1,0:T(8,128)(2,1)S(1)}, bf16[256,2048]{1,0:T(8,128)(2,1)S(1)}, u32[]{:S(2)}, u32[]{:S(2)}) collective-permute-start(bf16[256,2048]{1,0:T(8,128)(2,1)S(1)} %add_convert_fusion.10), channel_id=1, source_target_pairs={{0,2},{1,3},{2,0},{3,1},{4,6},{5,7},{6,4},{7,5},{8,10},{9,11},{10,... | collective-permute-start | bytes 3145736 | tf_op jit(solution)/shard_map/ppermute | solution.py:51
  287.1 191.8 %reduce-scatter.7.cloned.1.call-start = ((), (), s32[]{:S(2)}) async-start(), calls=%async_computation.9 | async-start | bytes 5242880 | tf_op jit(solution)/shard_map/reduce_scatter | solution.py:461
  291.9 26.1 %collective-permute-start.42 = (bf16[256,2048]{1,0:T(8,128)(2,1)}, bf16[256,2048]{1,0:T(8,128)(2,1)}, u32[]{:S(2)}, u32[]{:S(2)}) collective-permute-start(bf16[256,2048]{1,0:T(8,128)(2,1)} %convolution_convert_fusion.15), channel_id=1, source_target_pairs={{0,1},{1,0},{2,3},{3,2},{4,5},{5,4},{6,7},{7,6},{8,9},{9,8},{10,11... | collective-permute-start | bytes 3145736 | tf_op jit(solution)/shard_map/ppermute | solution.py:51
  295.6 26.4 %collective-permute-start.38 = (bf16[128,2048]{1,0:T(8,128)(2,1)}, bf16[128,2048]{1,0:T(8,128)(2,1)}, u32[]{:S(2)}, u32[]{:S(2)}) collective-permute-start(bf16[128,2048]{1,0:T(8,128)(2,1)} %get-tuple-element.263), channel_id=1, source_target_pairs={{0,4},{1,5},{2,6},{3,7},{4,0},{5,1},{6,2},{7,3},{8,12},{9,13},{10,... | collective-permute-start | bytes 1572872 | tf_op jit(solution)/shard_map/ppermute | solution.py:51
  345.7 156.6 %reduce-scatter.9.cloned.1.call-start = ((), (), s32[]{:S(2)}) async-start(), calls=%async_computation.10 | async-start | bytes 1310720 | tf_op jit(solution)/shard_map/reduce_scatter | solution.py:461
  357.9 25.5 %collective-permute-start.46 = (bf16[256,2048]{1,0:T(8,128)(2,1)S(1)}, bf16[256,2048]{1,0:T(8,128)(2,1)S(1)}, u32[]{:S(2)}, u32[]{:S(2)}) collective-permute-start(bf16[256,2048]{1,0:T(8,128)(2,1)S(1)} %fusion.70.refs_0_), channel_id=1, source_target_pairs={{0,4},{1,5},{2,6},{3,7},{4,0},{5,1},{6,2},{7,3},{8,12},{9,13},{10,... | collective-permute-start | bytes 3145736 | tf_op jit(solution)/shard_map/ppermute | solution.py:51
  359.4 25.2 %collective-permute-start.45 = (bf16[256,2048]{1,0:T(8,128)(2,1)S(1)}, bf16[256,2048]{1,0:T(8,128)(2,1)S(1)}, u32[]{:S(2)}, u32[]{:S(2)}) collective-permute-start(bf16[256,2048]{1,0:T(8,128)(2,1)S(1)} %fusion.70.refs_0_), channel_id=1, source_target_pairs={{0,2},{1,3},{2,0},{3,1},{4,6},{5,7},{6,4},{7,5},{8,10},{9,11},{10,... | collective-permute-start | bytes 3145736 | tf_op jit(solution)/shard_map/ppermute | solution.py:51
  402.0 34.6 %collective-permute-start.57 = (bf16[128,2048]{1,0:T(8,128)(2,1)}, bf16[128,2048]{1,0:T(8,128)(2,1)}, u32[]{:S(2)}, u32[]{:S(2)}) collective-permute-start(bf16[128,2048]{1,0:T(8,128)(2,1)} %get-tuple-element.165), channel_id=1, source_target_pairs={{0,2},{1,3},{2,0},{3,1},{4,6},{5,7},{6,4},{7,5},{8,10},{9,11},{10,... | collective-permute-start | bytes 1572872 | tf_op jit(solution)/shard_map/ppermute | solution.py:51
  402.9 33.7 %collective-permute-start.58 = (bf16[128,2048]{1,0:T(8,128)(2,1)}, bf16[128,2048]{1,0:T(8,128)(2,1)}, u32[]{:S(2)}, u32[]{:S(2)}) collective-permute-start(bf16[128,2048]{1,0:T(8,128)(2,1)} %get-tuple-element.166), channel_id=1, source_target_pairs={{0,4},{1,5},{2,6},{3,7},{4,0},{5,1},{6,2},{7,3},{8,12},{9,13},{10,... | collective-permute-start | bytes 1572872 | tf_op jit(solution)/shard_map/ppermute | solution.py:51
  403.5 33.1 %collective-permute-start.59 = (bf16[128,2048]{1,0:T(8,128)(2,1)}, bf16[128,2048]{1,0:T(8,128)(2,1)}, u32[]{:S(2)}, u32[]{:S(2)}) collective-permute-start(bf16[128,2048]{1,0:T(8,128)(2,1)} %get-tuple-element.167), channel_id=1, source_target_pairs={{0,2},{1,3},{2,0},{3,1},{4,6},{5,7},{6,4},{7,5},{8,10},{9,11},{10,... | collective-permute-start | bytes 1572872 | tf_op jit(solution)/shard_map/ppermute | solution.py:51
  404.6 32.0 %collective-permute-start.60 = (bf16[128,2048]{1,0:T(8,128)(2,1)}, bf16[128,2048]{1,0:T(8,128)(2,1)}, u32[]{:S(2)}, u32[]{:S(2)}) collective-permute-start(bf16[128,2048]{1,0:T(8,128)(2,1)} %get-tuple-element.168), channel_id=1, source_target_pairs={{0,4},{1,5},{2,6},{3,7},{4,0},{5,1},{6,2},{7,3},{8,12},{9,13},{10,... | collective-permute-start | bytes 1572872 | tf_op jit(solution)/shard_map/ppermute | solution.py:51
  450.0 114.1 %reduce-scatter.11.cloned.1.call-start = ((), (), s32[]{:S(2)}) async-start(), calls=%async_computation.11 | async-start | bytes 3932160 | tf_op jit(solution)/shard_map/reduce_scatter | solution.py:461
  (128 other events, 1484.5 us)
Sparse Core Ops, SparseCore 0:
  10.2 66.1 all-gather.4
  77.9 26.6 all-gather.6
  106.2 80.1 all-gather.10
  187.8 79.2 all-gather.8
  287.2 75.2 reduce-scatter.4
  364.7 77.2 reduce-scatter.6
  450.2 31.4 reduce-scatter.8
  495.2 68.8 reduce-scatter.10
where the time goes:
time: 581 us; the launch traced here: 574 us
  waiting for transfers between devices  218 us (38%)
  matrix products  148 us (25%)
  starting transfers between devices  66.5 us (11%)
  local copies, waits for them, and re-layouts  48.1 us (8%)
  Pallas kernels  46.7 us (8%)
  other arithmetic  30.6 us (5%)
  between operations  15.8 us (3%)
    ppermute x72, waiting for transfers between devices, exchange(): return lax.ppermute(piece, 'tp', [(at, at ^ mask) for at in range(SWAP_TP)])  167 us
    dot_general x13, matrix products, contract_cols(): lax.dot_general(left, right, (((1,), (1,)), ((), ())), preferred_element_...  57.4 us
    ppermute x72, starting transfers between devices, exchange(): return lax.ppermute(piece, 'tp', [(at, at ^ mask) for at in range(SWAP_TP)])  52.3 us
    dot_general x3, matrix products, contract_rows(): lax.dot_general(left, right, (((0,), (0,)), ((), ())), preferred_element_...  35 us
    unnamed x165, local copies, waits for them, and re-layouts  31.2 us
    all_gather x1, waiting for transfers between devices, gather_weights(): lax.all_gather(down_weight, 'fsdp', axis=1, tiled=True)  21.4 us
    pallas_call x1, Pallas kernels, attend_back(): pl.pallas_call(attend_back_kernel, out_shape=(jax.ShapeDtypeStruct(qkv_ro...  18.9 us
    dot_general x1, matrix products, layer(): jnp.dot(norm_piece, up_full, preferred_element_type=jnp.float32) + up_bias  18.3 us
  transfers between devices with their start and end apart: 87, of which 35 were waited for; matrix products, arithmetic and copies ran while one was open for 35% of the time, Pallas kernels for 8%

commit v1 on v0

--- a/solution.py
+++ b/solution.py
@@ -153,6 +153,22 @@
         + jnp.concatenate([x_low, x_high], axis=0)
         + jnp.concatenate([y_low, y_high], axis=0)
     )
+
+
+def scatter_tail(far_sums, left, multiply):
+    mixed, left = tie(scatter_pair(left, multiply, 1, 2), left)
+    half = mixed.shape[0] // 4
+    x_low, x_high, y_low, y_high = (mixed[at * half : (at + 1) * half] for at in range(4))
+    low_sums = exchange(x_low, 2), exchange(y_high, 4)
+    sums = scatter_second((*far_sums, *low_sums, x_high, y_low, mixed))[:4]
+    home = scatter_pair(left, multiply, 0, 1)
+    return scatter_last((*sums, home))
+
+
+def far_sends(left, multiply):
+    far, left = tie(scatter_pair(left, multiply, 3, 1), left)
+    half = far.shape[0] // 2
+    return (exchange(far[:half], 2), exchange(far[half:], 4)), left
 
 
 def sum_direct(vector, axis, steps):
@@ -499,14 +515,18 @@
     act_grad = contract_cols(grad_piece, down_full)
     pre_grad = (act_grad * slope.astype(jnp.float32)).astype(jnp.bfloat16)
     shift_acc = jnp.sum(pre_grad.astype(jnp.float32), axis=0)
-    norm2_grad_state = scatter_first(
-        scatter_multiply(
-            pre_grad, lambda part: contract_cols(part, up_full).astype(jnp.bfloat16)
-        )
-    )
+    split = lax.axis_size("tp") == SWAP_TP
+
+    def norm2_multiply(part):
+        return contract_cols(part, up_full).astype(jnp.bfloat16)
+
+    if split:
+        far_sums, rest = far_sends(pre_grad, norm2_multiply)
+        norm2_grad = scatter_tail(far_sums, rest, norm2_multiply)
+    else:
+        norm2_grad = scatter_last(scatter_first(scatter_multiply(pre_grad, norm2_multiply)))
     up_acc = contract_rows(norm_piece, pre_grad).astype(jnp.bfloat16)
-    norm2_grad_state, up_acc = tie(norm2_grad_state, up_acc)
-    norm2_grad = scatter_last(scatter_second(norm2_grad_state))
+    up_acc, norm2_grad = tie(up_acc, norm2_grad)
     _, ln2_back = jax.vjp(layer_norm, middle, ln2_gain, ln2_bias)
     middle_ln, grad_g2, grad_b2 = ln2_back(norm2_grad)
     grad_rows = out_grad.astype(jnp.float32)
@@ -537,24 +557,16 @@
     def norm1_multiply(part):
         return contract_cols(part, qkv_flat).astype(jnp.bfloat16)
 
-    split = lax.axis_size("tp") == SWAP_TP
     if split:
-        far = scatter_pair(qkv_grad, norm1_multiply, 3, 1)
-        far, qkv_grad = tie(far, qkv_grad)
-        mixed = scatter_pair(qkv_grad, norm1_multiply, 1, 2)
-        mixed, qkv_grad = tie(mixed, qkv_grad)
-        *norm1_state, home = scatter_send(scatter_pieces((far, mixed, mixed)))
-    else:
-        norm1_state = list(scatter_first(scatter_multiply(qkv_grad, norm1_multiply)))
+        far_sums, qkv_grad = far_sends(qkv_grad, norm1_multiply)
     grad_qkv_w = contract_rows(qkv_grad, norm1_rows).astype(jnp.bfloat16)
     grad_qkv_w, qkv_grad, shard_up = tie(grad_qkv_w, qkv_grad, shard_up)
-    norm1_state, qkv_grad, mlp_state = tie(norm1_state, qkv_grad, mlp_state)
     if split:
-        norm1_state = (*norm1_state, scatter_pair(qkv_grad, norm1_multiply, 0, 1))
-    norm1_state = tuple(norm1_state)
+        norm1_grad = scatter_tail(far_sums, qkv_grad, norm1_multiply)
+    else:
+        norm1_grad = scatter_last(scatter_first(scatter_multiply(qkv_grad, norm1_multiply)))
+    norm1_grad, shard_out, mlp_state = tie(norm1_grad, shard_out, mlp_state)
     layer_out = (middle + scatter_last(mlp_state) + down_bias).astype(jnp.bfloat16)
-    norm1_state, shard_out = tie(norm1_state, shard_out)
-    norm1_grad = scatter_last(scatter_second(norm1_state))
     shard_qkv = sum_weights(grad_qkv_w, 1).reshape(3, head_cols, -1).transpose(2, 0, 1)
     _, ln1_back = jax.vjp(layer_norm, inputs, ln1_gain, ln1_bias)
     input_ln, grad_g1, grad_b1 = ln1_back(norm1_grad)

time: 581 us -> 570 us (0.981)
    unnamed x165 -> x139, local copies, waits for them, and re-layouts: 31.2 us -> 28.9 us
  transfers between devices with their start and end apart: 87 -> 87, of which waited for: 35 -> 38; matrix products, arithmetic and copies ran while one was open for 35% -> 34% of each run, Pallas kernels for 8% -> 8%
where the time goes in v1:
time: 570 us; the launch traced here: 563 us
  waiting for transfers between devices  215 us (38%)
  matrix products  147 us (26%)
  starting transfers between devices  67 us (12%)
  Pallas kernels  46.6 us (8%)
  local copies, waits for them, and re-layouts  45.4 us (8%)
  other arithmetic  25.6 us (4%)
  between operations  15.7 us (3%)
    ppermute x72, waiting for transfers between devices, exchange(): return lax.ppermute(piece, 'tp', [(at, at ^ mask) for at in range(SWAP_TP)])  172 us
    dot_general x13, matrix products, contract_cols(): lax.dot_general(left, right, (((1,), (1,)), ((), ())), preferred_element_...  56.8 us
    ppermute x72, starting transfers between devices, exchange(): return lax.ppermute(piece, 'tp', [(at, at ^ mask) for at in range(SWAP_TP)])  52.1 us
    dot_general x3, matrix products, contract_rows(): lax.dot_general(left, right, (((0,), (0,)), ((), ())), preferred_element_...  34.6 us
    unnamed x139, local copies, waits for them, and re-layouts  28.9 us
    all_gather x1, waiting for transfers between devices, gather_weights(): lax.all_gather(down_weight, 'fsdp', axis=1, tiled=True)  21.5 us
    pallas_call x1, Pallas kernels, attend_back(): pl.pallas_call(attend_back_kernel, out_shape=(jax.ShapeDtypeStruct(qkv_ro...  18.9 us
    dot_general x1, matrix products, layer(): jnp.dot(norm_piece, up_full, preferred_element_type=jnp.float32) + up_bias  18.3 us
  transfers between devices with their start and end apart: 87, of which 38 were waited for; matrix products, arithmetic and copies ran while one was open for 34% of the time, Pallas kernels for 8%

profile of v1, /device:TPU:0, one launch (start us, length us, event | category | flops | bytes accessed | tf_op | source)
XLA Modules:
  0.0 562.5 jit_solution(16375922669841547034)
XLA Ops:
  17.6 21.8 %collective-permute-done.1 = bf16[256,2048]{1,0:T(8,128)(2,1)S(1)} collective-permute-done((bf16[256,2048]{1,0:T(8,128)(2,1)}, bf16[256,2048]{1,0:T(8,128)(2,1)S(1)}, u32[]{:S(2)}, u32[]{:S(2)}) %collective-permute-start.1) | collective-permute-done | bytes 1048608 | tf_op jit(solution)/shard_map/ppermute | solution.py:51
  45.7 7.1 %collective-permute-done.3 = bf16[128,2048]{1,0:T(8,128)(2,1)S(1)} collective-permute-done((bf16[128,2048]{1,0:T(8,128)(2,1)S(1)}, bf16[128,2048]{1,0:T(8,128)(2,1)S(1)}, u32[]{:S(2)}, u32[]{:S(2)}) %collective-permute-start.3) | collective-permute-done | bytes 524320 | tf_op jit(solution)/shard_map/ppermute | solution.py:51
  63.1 13.3 %all-gather.5.cloned.1.call-done = bf16[2048,3,256]{0,2,1:T(8,128)(2,1)} async-done(((bf16[512,3,256]{0,2,1:T(8,128)(2,1)}), bf16[2048,3,256]{0,2,1:T(8,128)(2,1)}) %all-gather.5.cloned.1.call-update) | async-done | bytes 3145744 | tf_op jit(solution)/shard_map/all_gather | solution.py:470
  76.4 11.3 %add_convert_fusion.1.qkv = bf16[2048,768]{1,0:T(8,128)(2,1)} fusion(f32[768]{0:T(1024)S(1)} %pad_maximum_fusion, bf16[2048,2048]{1,0:T(8,128)(2,1)} %constant_dynamic-update-slice_fusion, bf16[2048,768]{0,1:T(8,128)(2,1)} %bitcast.55), kind=kOutput, calls=%fused_computation.6 | convolution fusion | flops 6445596672 | bytes 14683136 | tf_op jit(solution)/shard_map/dot_general | solution.py:490
  94.9 16.2 %attend.1 = (bf16[2048,256]{1,0:T(8,128)(2,1)}, f32[16,2048]{1,0:T(8,128)}) custom-call(s32[3,8]{1,0:T(4,128)} %pad_add_fusion.table, bf16[2048,768]{1,0:T(8,128)(2,1)} %add_convert_fusion.1.qkv), custom_call_target="tpu_custom_call" | custom-call | tf_op jit(solution)/shard_map/attend/pallas_call | solution.py:368
  127.2 9.3 %collective-permute-done.22 = bf16[128,2048]{1,0:T(8,128)(2,1)S(1)} collective-permute-done((bf16[128,2048]{1,0:T(8,128)(2,1)S(1)}, bf16[128,2048]{1,0:T(8,128)(2,1)S(1)}, u32[]{:S(2)}, u32[]{:S(2)}) %collective-permute-start.22) | collective-permute-done | bytes 524320 | tf_op jit(solution)/shard_map/ppermute | solution.py:51
  143.7 8.2 %collective-permute-done.23 = bf16[128,2048]{1,0:T(8,128)(2,1)S(1)} collective-permute-done((bf16[128,2048]{1,0:T(8,128)(2,1)S(1)}, bf16[128,2048]{1,0:T(8,128)(2,1)S(1)}, u32[]{:S(2)}, u32[]{:S(2)}) %collective-permute-start.23) | collective-permute-done | bytes 524320 | tf_op jit(solution)/shard_map/ppermute | solution.py:51
  152.4 9.0 %collective-permute-done.24 = bf16[128,2048]{1,0:T(8,128)(2,1)S(1)} collective-permute-done((bf16[128,2048]{1,0:T(8,128)(2,1)S(1)}, bf16[128,2048]{1,0:T(8,128)(2,1)S(1)}, u32[]{:S(2)}, u32[]{:S(2)}) %collective-permute-start.24) | collective-permute-done | bytes 524320 | tf_op jit(solution)/shard_map/ppermute | solution.py:51
  170.4 19.7 %collective-permute-done.28 = bf16[256,2048]{1,0:T(8,128)(2,1)S(1)} collective-permute-done((bf16[256,2048]{1,0:T(8,128)(2,1)S(1)}, bf16[256,2048]{1,0:T(8,128)(2,1)S(1)}, u32[]{:S(2)}, u32[]{:S(2)}) %collective-permute-start.28) | collective-permute-done | bytes 1048608 | tf_op jit(solution)/shard_map/ppermute | solution.py:51
  197.1 10.1 %collective-permute-done.30 = bf16[128,2048]{1,0:T(8,128)(2,1)S(1)} collective-permute-done((bf16[128,2048]{1,0:T(8,128)(2,1)S(1)}, bf16[128,2048]{1,0:T(8,128)(2,1)S(1)}, u32[]{:S(2)}, u32[]{:S(2)}) %collective-permute-start.30) | collective-permute-done | bytes 524320 | tf_op jit(solution)/shard_map/ppermute | solution.py:51
  214.2 18.3 %add_convert_fusion = (bf16[2048,1024]{1,0:T(8,128)(2,1)}, bf16[2048,1024]{1,0:T(8,128)(2,1)S(1)}) fusion(f32[1024]{0:T(1024)S(1)} %copy-done.47, bf16[2048,2048]{1,0:T(8,128)(2,1)} %constant_dynamic-update-slice_fusion.20, bf16[2048,1024]{1,0:T(8,128)(2,1)} %all-gather.11.cloned.1.call-done), kind=kOutput, calls=%fused_computation.2 | convolution fusion | flops 8631877632 | bytes 20975616 | tf_op jit(solution)/shard_map/dot_general | solution.py:509
  234.5 11.0 %convolution_convert_fusion = bf16[1024,2048]{1,0:T(8,128)(2,1)} fusion(bf16[2048,1024]{1,0:T(8,128)(2,1)S(1)} %get-tuple-element.135, bf16[2048,2048]{1,0:T(8,128)(2,1)S(1)} %copy-done.25), kind=kOutput, calls=%fused_computation.11 | convolution fusion | flops 8592031744 | bytes 16777216 | tf_op jit(solution)/shard_map/dot_general | solution.py:32
  245.5 21.5 %all-gather.9.cloned.1.call-done = bf16[1024,2048]{1,0:T(8,128)(2,1)} async-done(((bf16[1024,512]{1,0:T(8,128)(2,1)}), bf16[1024,2048]{1,0:T(8,128)(2,1)}) %all-gather.9.cloned.1.call-update) | async-done | bytes 4194320 | tf_op jit(solution)/shard_map/all_gather | solution.py:473
  267.1 13.5 %convert_reduce_fusion = (f32[1024]{0:T(1024)S(1)}, bf16[2048,1024]{1,0:T(8,128)(2,1)S(1)}) fusion(bf16[2048,1024]{1,0:T(8,128)(2,1)} %get-tuple-element.128, bf16[2048,2048]{1,0:T(8,128)(2,1)} %copy-done.24, bf16[1024,2048]{1,0:T(8,128)(2,1)} %all-gather.9.cloned.1.call-done), kind=kOutput, calls=%fused_computation | convolution fusion | flops 8600419328 | bytes 20975616 | tf_op jit(solution)/shard_map/dot_general | solution.py:38
  313.6 12.9 %convolution_convert_fusion.1 = bf16[2048,1024]{1,0:T(8,128)(2,1)} fusion(bf16[2048,2048]{1,0:T(8,128)(2,1)} %constant_dynamic-update-slice_fusion.20, bf16[2048,1024]{1,0:T(8,128)(2,1)S(1)} %copy-done.49), kind=kOutput, calls=%fused_computation.12 | convolution fusion | flops 8592031744 | bytes 16777216 | tf_op jit(solution)/shard_map/dot_general | solution.py:32
  363.4 14.7 %collective-permute-done.46.refs_2_ = bf16[256,2048]{1,0:T(8,128)(2,1)} collective-permute-done((bf16[256,2048]{1,0:T(8,128)(2,1)S(1)}, bf16[256,2048]{1,0:T(8,128)(2,1)}, u32[]{:S(2)}, u32[]{:S(2)}) %collective-permute-start.46) | collective-permute-done | bytes 1048608 | tf_op jit(solution)/shard_map/ppermute | solution.py:51
  383.1 9.6 %collective-permute-done.52.refs_4_ = bf16[128,2048]{1,0:T(8,128)(2,1)} collective-permute-done((bf16[128,2048]{1,0:T(8,128)(2,1)S(1)}, bf16[128,2048]{1,0:T(8,128)(2,1)}, u32[]{:S(2)}, u32[]{:S(2)}) %collective-permute-start.52) | collective-permute-done | bytes 524320 | tf_op jit(solution)/shard_map/ppermute | solution.py:51
  400.5 11.5 %project_back.1 = (bf16[2048,256]{1,0:T(8,128)(2,1)}, bf16[256,2048]{1,0:T(8,128)(2,1)}) custom-call(bf16[256,2048]{1,0:T(8,128)(2,1)} %copy-done.11, bf16[256,2048]{1,0:T(8,128)(2,1)} %collective-permute-done.45.refs_1_, bf16[256,2048]{1,0:T(8,128)(2,1)} %collective-permute-done.46.refs_2_, bf16[128,2048]{1,0:T(8,128)(2,1)} %collective-permute-done.51.refs_3_, ...), custom_call_target="tpu_custom_call" | custom-call | tf_op jit(solution)/shard_map/project_back/pallas_call | solution.py:425
  412.0 18.9 %attend_back.1 = (bf16[2048,768]{1,0:T(8,128)(2,1)}, f32[8,256]{1,0:T(8,128)}) custom-call(s32[3,8]{1,0:T(4,128)} %pad_add_fusion.table, bf16[2048,768]{1,0:T(8,128)(2,1)} %add_convert_fusion.1.qkv, bf16[2048,256]{1,0:T(8,128)(2,1)} %get-tuple-element.112.refs_10_.ctx, bf16[2048,256]{1,0:T(8,128)(2,1)} %get-tuple-element.165.ctx_grad, ...), custom_call_target="tpu_custom_call" | custom-call | tf_op jit(solution)/shard_map/attend_back/pallas_call | solution.py:382
  441.8 10.6 %convolution_convert_fusion.2 = bf16[768,2048]{1,0:T(8,128)(2,1)} fusion(bf16[2048,768]{1,0:T(8,128)(2,1)S(1)} %copy-done.45, bf16[2048,2048]{1,0:T(8,128)(2,1)} %constant_dynamic-update-slice_fusion), kind=kOutput, calls=%fused_computation.13 | convolution fusion | flops 6444023808 | bytes 14680064 | tf_op jit(solution)/shard_map/dot_general | solution.py:32
  485.6 7.3 %collective-permute-done.68 = bf16[128,2048]{1,0:T(8,128)(2,1)S(1)} collective-permute-done((bf16[128,2048]{1,0:T(8,128)(2,1)S(1)}, bf16[128,2048]{1,0:T(8,128)(2,1)S(1)}, u32[]{:S(2)}, u32[]{:S(2)}) %collective-permute-start.68) | collective-permute-done | bytes 524320 | tf_op jit(solution)/shard_map/ppermute | solution.py:51
  495.7 8.5 %collective-permute-done.69 = bf16[128,2048]{1,0:T(8,128)(2,1)S(1)} collective-permute-done((bf16[128,2048]{1,0:T(8,128)(2,1)S(1)}, bf16[128,2048]{1,0:T(8,128)(2,1)S(1)}, u32[]{:S(2)}, u32[]{:S(2)}) %collective-permute-start.69) | collective-permute-done | bytes 524320 | tf_op jit(solution)/shard_map/ppermute | solution.py:51
  522.3 9.7 %collective-permute-start.73 = (f32[13824]{0:T(1024)S(1)}, f32[13824]{0:T(1024)S(1)}, u32[]{:S(2)}, u32[]{:S(2)}) collective-permute-start(f32[13824]{0:T(1024)S(1)} %constant_dynamic-update-slice_fusion.31), channel_id=1, source_target_pairs={{0,16},{8,24},{16,0},{24,8},{1,17},{9,25},{17,1},{25,9},{2,18},{10... | collective-permute-start | bytes 165896 | tf_op jit(solution)/shard_map/ppermute | solution.py:177
  532.0 8.0 %collective-permute-done.73 = f32[13824]{0:T(1024)S(1)} collective-permute-done((f32[13824]{0:T(1024)S(1)}, f32[13824]{0:T(1024)S(1)}, u32[]{:S(2)}, u32[]{:S(2)}) %collective-permute-start.73) | collective-permute-done | bytes 55328 | tf_op jit(solution)/shard_map/ppermute | solution.py:177
  (397 shorter events, 244.9 us)
Async XLA Ops:
  7.2 69.1 %all-gather.5.cloned.1.call-start = ((), (), s32[]{:S(2)}) async-start(), calls=%async_computation.4 | async-start | bytes 3932160 | tf_op jit(solution)/shard_map/all_gather | solution.py:470
  9.7 101.5 %all-gather.7.cloned.1.call-start = ((), (), s32[]{:S(2)}) async-start(), calls=%async_computation.5 | async-start | bytes 1310720 | tf_op jit(solution)/shard_map/all_gather | solution.py:471
  10.4 203.8 %all-gather.11.cloned.1.call-start = ((), (), s32[]{:S(2)}) async-start(), calls=%async_computation.7 | async-start | bytes 5242880 | tf_op jit(solution)/shard_map/all_gather | solution.py:472
  13.0 26.4 %collective-permute-start.1 = (bf16[256,2048]{1,0:T(8,128)(2,1)}, bf16[256,2048]{1,0:T(8,128)(2,1)S(1)}, u32[]{:S(2)}, u32[]{:S(2)}) collective-permute-start(bf16[256,2048]{1,0:T(8,128)(2,1)} %get-tuple-element.210), channel_id=1, source_target_pairs={{0,4},{1,5},{2,6},{3,7},{4,0},{5,1},{6,2},{7,3},{8,12},{9,13},{10,... | collective-permute-start | bytes 3145736 | tf_op jit(solution)/shard_map/ppermute | solution.py:51
  16.1 25.2 %collective-permute-start = (bf16[256,2048]{1,0:T(8,128)(2,1)}, bf16[256,2048]{1,0:T(8,128)(2,1)S(1)}, u32[]{:S(2)}, u32[]{:S(2)}) collective-permute-start(bf16[256,2048]{1,0:T(8,128)(2,1)} %get-tuple-element.210), channel_id=1, source_target_pairs={{0,2},{1,3},{2,0},{3,1},{4,6},{5,7},{6,4},{7,5},{8,10},{9,11},{10,... | collective-permute-start | bytes 3145736 | tf_op jit(solution)/shard_map/ppermute | solution.py:51
  17.5 38.1 %collective-permute-start.4 = (bf16[256,2048]{1,0:T(8,128)(2,1)}, bf16[256,2048]{1,0:T(8,128)(2,1)S(1)}, u32[]{:S(2)}, u32[]{:S(2)}) collective-permute-start(bf16[256,2048]{1,0:T(8,128)(2,1)} %get-tuple-element.210), channel_id=1, source_target_pairs={{0,1},{1,0},{2,3},{3,2},{4,5},{5,4},{6,7},{7,6},{8,9},{9,8},{10,11... | collective-permute-start | bytes 3145736 | tf_op jit(solution)/shard_map/ppermute | solution.py:51
  17.6 249.5 %all-gather.9.cloned.1.call-start = ((), (), s32[]{:S(2)}) async-start(), calls=%async_computation.6 | async-start | bytes 5242880 | tf_op jit(solution)/shard_map/all_gather | solution.py:473
  60.5 27.1 %collective-permute-start.11 = (bf16[256,2048]{1,0:T(8,128)(2,1)S(1)}, bf16[256,2048]{1,0:T(8,128)(2,1)S(1)}, u32[]{:S(2)}, u32[]{:S(2)}) collective-permute-start(bf16[256,2048]{1,0:T(8,128)(2,1)S(1)} %copy-done.7), channel_id=1, source_target_pairs={{0,1},{1,0},{2,3},{3,2},{4,5},{5,4},{6,7},{7,6},{8,9},{9,8},{10,11... | collective-permute-start | bytes 3145736 | tf_op jit(solution)/shard_map/ppermute | solution.py:51
  61.0 26.6 %collective-permute-start.10 = (bf16[256,2048]{1,0:T(8,128)(2,1)S(1)}, bf16[256,2048]{1,0:T(8,128)(2,1)S(1)}, u32[]{:S(2)}, u32[]{:S(2)}) collective-permute-start(bf16[256,2048]{1,0:T(8,128)(2,1)S(1)} %copy-done.7), channel_id=1, source_target_pairs={{0,4},{1,5},{2,6},{3,7},{4,0},{5,1},{6,2},{7,3},{8,12},{9,13},{10,... | collective-permute-start | bytes 3145736 | tf_op jit(solution)/shard_map/ppermute | solution.py:51
  62.6 25.1 %collective-permute-start.9 = (bf16[256,2048]{1,0:T(8,128)(2,1)S(1)}, bf16[256,2048]{1,0:T(8,128)(2,1)}, u32[]{:S(2)}, u32[]{:S(2)}) collective-permute-start(bf16[256,2048]{1,0:T(8,128)(2,1)S(1)} %copy-done.7), channel_id=1, source_target_pairs={{0,2},{1,3},{2,0},{3,1},{4,6},{5,7},{6,4},{7,5},{8,10},{9,11},{10,... | collective-permute-start | bytes 3145736 | tf_op jit(solution)/shard_map/ppermute | solution.py:51
  116.7 277.4 %reduce-scatter.5.cloned.1.call-start = ((), (), s32[]{:S(2)}) async-start(), calls=%async_computation.8 | async-start | bytes 5242880 | tf_op jit(solution)/shard_map/reduce_scatter | solution.py:477
  117.6 26.0 %collective-permute-start.16 = (bf16[256,2048]{1,0:T(8,128)(2,1)S(1)}, bf16[256,2048]{1,0:T(8,128)(2,1)S(1)}, u32[]{:S(2)}, u32[]{:S(2)}) collective-permute-start(bf16[256,2048]{1,0:T(8,128)(2,1)S(1)} %convolution_convert_fusion.21), channel_id=1, source_target_pairs={{0,1},{1,0},{2,3},{3,2},{4,5},{5,4},{6,7},{7,6},{8,9},{9,8},{10,11... | collective-permute-start | bytes 3145736 | tf_op jit(solution)/shard_map/ppermute | solution.py:51
  143.6 26.6 %collective-permute-start.25 = (bf16[128,2048]{1,0:T(8,128)(2,1)}, bf16[128,2048]{1,0:T(8,128)(2,1)S(1)}, u32[]{:S(2)}, u32[]{:S(2)}) collective-permute-start(bf16[128,2048]{1,0:T(8,128)(2,1)} %collective-permute-done.12), channel_id=1, source_target_pairs={{0,1},{1,0},{2,3},{3,2},{4,5},{5,4},{6,7},{7,6},{8,9},{9,8},{10,11... | collective-permute-start | bytes 1572872 | tf_op jit(solution)/shard_map/ppermute | solution.py:51
  164.5 25.6 %collective-permute-start.28 = (bf16[256,2048]{1,0:T(8,128)(2,1)S(1)}, bf16[256,2048]{1,0:T(8,128)(2,1)S(1)}, u32[]{:S(2)}, u32[]{:S(2)}) collective-permute-start(bf16[256,2048]{1,0:T(8,128)(2,1)S(1)} %add_convert_fusion.11), channel_id=1, source_target_pairs={{0,4},{1,5},{2,6},{3,7},{4,0},{5,1},{6,2},{7,3},{8,12},{9,13},{10,... | collective-permute-start | bytes 3145736 | tf_op jit(solution)/shard_map/ppermute | solution.py:51
  166.1 25.2 %collective-permute-start.27 = (bf16[256,2048]{1,0:T(8,128)(2,1)S(1)}, bf16[256,2048]{1,0:T(8,128)(2,1)S(1)}, u32[]{:S(2)}, u32[]{:S(2)}) collective-permute-start(bf16[256,2048]{1,0:T(8,128)(2,1)S(1)} %add_convert_fusion.11), channel_id=1, source_target_pairs={{0,2},{1,3},{2,0},{3,1},{4,6},{5,7},{6,4},{7,5},{8,10},{9,11},{10,... | collective-permute-start | bytes 3145736 | tf_op jit(solution)/shard_map/ppermute | solution.py:51
  289.8 162.8 %reduce-scatter.7.cloned.1.call-start = ((), (), s32[]{:S(2)}) async-start(), calls=%async_computation.9 | async-start | bytes 5242880 | tf_op jit(solution)/shard_map/reduce_scatter | solution.py:477
  340.1 174.8 %reduce-scatter.9.cloned.1.call-start = ((), (), s32[]{:S(2)}) async-start(), calls=%async_computation.10 | async-start | bytes 1310720 | tf_op jit(solution)/shard_map/reduce_scatter | solution.py:477
  352.4 25.7 %collective-permute-start.46 = (bf16[256,2048]{1,0:T(8,128)(2,1)S(1)}, bf16[256,2048]{1,0:T(8,128)(2,1)}, u32[]{:S(2)}, u32[]{:S(2)}) collective-permute-start(bf16[256,2048]{1,0:T(8,128)(2,1)S(1)} %fusion.70.refs_0_), channel_id=1, source_target_pairs={{0,4},{1,5},{2,6},{3,7},{4,0},{5,1},{6,2},{7,3},{8,12},{9,13},{10,... | collective-permute-start | bytes 3145736 | tf_op jit(solution)/shard_map/ppermute | solution.py:51
  353.0 25.3 %collective-permute-start.45 = (bf16[256,2048]{1,0:T(8,128)(2,1)S(1)}, bf16[256,2048]{1,0:T(8,128)(2,1)}, u32[]{:S(2)}, u32[]{:S(2)}) collective-permute-start(bf16[256,2048]{1,0:T(8,128)(2,1)S(1)} %fusion.70.refs_0_), channel_id=1, source_target_pairs={{0,2},{1,3},{2,0},{3,1},{4,6},{5,7},{6,4},{7,5},{8,10},{9,11},{10,... | collective-permute-start | bytes 3145736 | tf_op jit(solution)/shard_map/ppermute | solution.py:51
  396.4 34.6 %collective-permute-start.57 = (bf16[128,2048]{1,0:T(8,128)(2,1)}, bf16[128,2048]{1,0:T(8,128)(2,1)}, u32[]{:S(2)}, u32[]{:S(2)}) collective-permute-start(bf16[128,2048]{1,0:T(8,128)(2,1)} %get-tuple-element.148), channel_id=1, source_target_pairs={{0,2},{1,3},{2,0},{3,1},{4,6},{5,7},{6,4},{7,5},{8,10},{9,11},{10,... | collective-permute-start | bytes 1572872 | tf_op jit(solution)/shard_map/ppermute | solution.py:51
  398.0 33.0 %collective-permute-start.58 = (bf16[128,2048]{1,0:T(8,128)(2,1)}, bf16[128,2048]{1,0:T(8,128)(2,1)}, u32[]{:S(2)}, u32[]{:S(2)}) collective-permute-start(bf16[128,2048]{1,0:T(8,128)(2,1)} %get-tuple-element.149), channel_id=1, source_target_pairs={{0,4},{1,5},{2,6},{3,7},{4,0},{5,1},{6,2},{7,3},{8,12},{9,13},{10,... | collective-permute-start | bytes 1572872 | tf_op jit(solution)/shard_map/ppermute | solution.py:51
  399.4 31.5 %collective-permute-start.59 = (bf16[128,2048]{1,0:T(8,128)(2,1)}, bf16[128,2048]{1,0:T(8,128)(2,1)}, u32[]{:S(2)}, u32[]{:S(2)}) collective-permute-start(bf16[128,2048]{1,0:T(8,128)(2,1)} %get-tuple-element.150), channel_id=1, source_target_pairs={{0,2},{1,3},{2,0},{3,1},{4,6},{5,7},{6,4},{7,5},{8,10},{9,11},{10,... | collective-permute-start | bytes 1572872 | tf_op jit(solution)/shard_map/ppermute | solution.py:51
  399.9 31.0 %collective-permute-start.60 = (bf16[128,2048]{1,0:T(8,128)(2,1)}, bf16[128,2048]{1,0:T(8,128)(2,1)}, u32[]{:S(2)}, u32[]{:S(2)}) collective-permute-start(bf16[128,2048]{1,0:T(8,128)(2,1)} %get-tuple-element.151), channel_id=1, source_target_pairs={{0,4},{1,5},{2,6},{3,7},{4,0},{5,1},{6,2},{7,3},{8,12},{9,13},{10,... | collective-permute-start | bytes 1572872 | tf_op jit(solution)/shard_map/ppermute | solution.py:51
  435.0 117.8 %reduce-scatter.11.cloned.1.call-start = ((), (), s32[]{:S(2)}) async-start(), calls=%async_computation.11 | async-start | bytes 3932160 | tf_op jit(solution)/shard_map/reduce_scatter | solution.py:477
  (115 other events, 1352.9 us)
Sparse Core Ops, SparseCore 0:
  10.2 66.1 all-gather.4
  77.9 26.6 all-gather.6
  106.2 80.1 all-gather.10
  187.8 79.2 all-gather.8
  289.9 75.3 reduce-scatter.4
  367.4 77.2 reduce-scatter.6
  447.0 27.7 reduce-scatter.8
  477.1 62.3 reduce-scatter.10
